TPU v7x, 32 devices: a whole 2x2x4 slice. The times are simulated.
32 devices in a mesh: tensor: 4 (over y, x), expert: 8 (over z, core).
Axes of the slice: x: 2, y: 2, z: 4, core: 2. Of those that a mesh axis runs over, the one named last changes fastest.
Arguments:
- tokens: bfloat16 [16, 1024, 768], P('expert', 'tensor'), may hold values from -6 to 6
- out_grad: bfloat16 [16, 1024, 768], P('expert', 'tensor'), may hold values from -6 to 6
- masked: int32 [16, 1024], P('expert', 'tensor'), may hold values from 0 to 1, as said below
- route: int32 [16, 1024, 1], P('expert', 'tensor'), may hold values from 0 to 3
- norm1_gain: float32 [768], replicated, may hold values from 0.5 to 1.5
- query_key_value_weight: bfloat16 [3, 768, 768], P(None, None, 'tensor'), may hold values from -0.625 to 0.625
- output_weight: bfloat16 [768, 768], P('tensor'), may hold values from -5 to 5
- norm2_gain: float32 [768], replicated, may hold values from 0.5 to 1.5
- route_weight: float32 [768, 16], replicated, may hold values from -0.21875 to 0.21875
- expert_embed: float32 [4, 16], replicated, may hold values from -6 to 6
- up_weight: bfloat16 [8, 768, 1536], P('expert'), may hold values from -0.21875 to 0.21875
- down_weight: bfloat16 [8, 768, 1536], P('expert'), may hold values from -1 to 1
Outputs:
- out: float32 [16, 1024, 768], P('expert', 'tensor')
- input_grad: float32 [16, 1024, 768], P('expert', 'tensor')
- loads: float32 [4], replicated
- norm1_grad: float32 [768], replicated
- query_key_value_gradient: float32 [3, 768, 768], P(None, None, 'tensor')
- out_proj_grad: float32 [768, 768], P('tensor')
- norm2_grad: float32 [768], replicated
- route_weight_grad: float32 [768, 16], replicated
- embed_grad: float32 [4, 16], replicated
- up_weight_grad: float32 [8, 768, 1536], P('expert', None, 'tensor')
- down_weight_grad: float32 [8, 768, 1536], P('expert', None, 'tensor')
Inputs may be any that keep to these rules, and one draw needn't show every extreme that they name: 1 marks a masked position; only these carry a gradient. Every expert is the route of some token.
All inputs are finite; a program needn't handle non-finite values.
Results may differ from a plain program's by a relative error of at most 0.015.
The roundings to bfloat16 on the way count: a program that leaves them out, or rounds other values in their place, can miss the bound.
Values may be sent and summed in bfloat16 or wider, within the bound.
No kernel may reach another device: no remote copies, remote signals or barrier semaphores. Data moves between devices by JAX's collectives and lax.ppermute only.
A program may use at most 192 MiB of HBM per device.

v0:
```python
from functools import partial
import jax
import jax.numpy as jnp
from jax import lax
from jax.sharding import PartitionSpec as P

HEAD = 64


def layer_norm(values, gain):
    center = values - jnp.mean(values, axis=-1, keepdims=True)
    spread = jnp.mean(center * center, axis=-1, keepdims=True)
    return center * lax.rsqrt(spread + 1e-05) * gain


def unit_rows(values):
    return values * lax.rsqrt(jnp.sum(values * values, axis=-1, keepdims=True) + 1e-06)


def gelu_exact(values):
    return jax.nn.gelu(values, approximate=False)


def pair_copy(values):
    count = values.shape[0]
    return jnp.broadcast_to(values[:, None], (count, 2) + values.shape[1:]).reshape(
        (2 * count,) + values.shape[1:]
    )


def pair_total(values):
    count = values.shape[0] // 2
    return jnp.sum(values.reshape((count, 2) + values.shape[1:]), axis=1)


def route_gate(normed, route_weight, expert_embed, picked):
    rows = unit_rows(jnp.dot(normed, route_weight, precision=lax.Precision.HIGHEST))
    centers = unit_rows(expert_embed)
    logits = 3.0 * jnp.dot(rows, centers.T, precision=lax.Precision.HIGHEST)
    probs = jax.nn.softmax(logits, axis=-1)
    return jnp.sum(probs * picked, axis=-1)


def attend_forward(query, key_all, value_all, score_scale):
    scores = (
        jnp.einsum("bhe,khe->hbk", query, key_all, preferred_element_type=jnp.float32) * score_scale
    )
    top = jnp.max(scores, axis=-1, keepdims=True)
    expos = jnp.exp(scores - top)
    total = jnp.sum(expos, axis=-1, keepdims=True)
    probs = (expos / total).astype(jnp.bfloat16)
    mixed = jnp.einsum("hbk,khe->bhe", probs, value_all, preferred_element_type=jnp.float32)
    return (mixed.astype(jnp.bfloat16), (top + jnp.log(total))[..., 0])


def attend_backward(query, key_all, value_all, grad_mixed, log_total, score_scale):
    scores = (
        jnp.einsum("bhe,khe->hbk", query, key_all, preferred_element_type=jnp.float32) * score_scale
    )
    probs = jnp.exp(scores - log_total[..., None])
    probs_low = probs.astype(jnp.bfloat16)
    grad_probs = jnp.einsum(
        "bhe,khe->hbk", grad_mixed, value_all, preferred_element_type=jnp.float32
    )
    inner = jnp.sum(probs * grad_probs, axis=-1, keepdims=True)
    grad_scores = (probs * (grad_probs - inner)).astype(jnp.bfloat16)
    query_part = (
        jnp.einsum("hbk,khe->bhe", grad_scores, key_all, preferred_element_type=jnp.float32)
        * score_scale
    )
    key_part = (
        jnp.einsum("hbk,bhe->khe", grad_scores, query, preferred_element_type=jnp.float32)
        * score_scale
    )
    value_part = jnp.einsum(
        "hbk,bhe->khe", probs_low, grad_mixed, preferred_element_type=jnp.float32
    )
    return (query_part, key_part, value_part)


def body(
    tokens,
    out_grad,
    masked,
    route,
    norm1_gain,
    query_key_value_weight,
    output_weight,
    norm2_gain,
    route_weight,
    expert_embed,
    up_weight,
    down_weight,
):
    seq_count, shard_len, features = tokens.shape
    rows_here = seq_count * shard_len
    experts = expert_embed.shape[0]
    capacity = rows_here // experts
    channels = query_key_value_weight.shape[2]
    head_count = channels // HEAD
    score_scale = HEAD ** (-0.5)
    contract_rows = (((0,), (0,)), ((), ()))
    contract_cols = (((1,), (1,)), ((), ()))
    inputs = tokens.astype(jnp.float32).reshape(rows_here, features)
    normed_one, norm_one_pull = jax.vjp(layer_norm, inputs, norm1_gain)
    normed_low = normed_one.astype(jnp.bfloat16).reshape(seq_count, shard_len, features)
    collected_rows = lax.all_gather(normed_low, "tensor", axis=1, tiled=True)
    seq_len = collected_rows.shape[1]
    block = min(512, seq_len)
    projected = jnp.einsum(
        "wxa,cam->cwxm", collected_rows, query_key_value_weight, preferred_element_type=jnp.float32
    ).astype(jnp.bfloat16)
    heads_view = projected.reshape(3, seq_count, seq_len, head_count, HEAD)
    mixed_seqs = []
    total_rows = []
    for sequence in range(seq_count):
        key_all = heads_view[1, sequence]
        value_all = heads_view[2, sequence]
        mixed_blocks = []
        total_blocks = []
        for start_row in range(0, seq_len, block):
            mixed_blk, total_blk = attend_forward(
                heads_view[0, sequence, start_row : start_row + block],
                key_all,
                value_all,
                score_scale,
            )
            mixed_blocks.append(mixed_blk)
            total_blocks.append(total_blk)
        mixed_seqs.append(jnp.concatenate(mixed_blocks, axis=0))
        total_rows.append(jnp.concatenate(total_blocks, axis=1))
    mixed_everything = jnp.stack(mixed_seqs, axis=0).reshape(seq_count, seq_len, channels)
    piece = mixed_everything
    attn = lax.psum_scatter(
        jnp.einsum("slh,hd->lsd", piece, output_weight, preferred_element_type=jnp.float32),
        "tensor",
        scatter_dimension=0,
        tiled=True,
    )
    hidden = inputs + attn.transpose(1, 0, 2).reshape(rows_here, features)
    normed_two, norm_two_pull = jax.vjp(layer_norm, hidden, norm2_gain)
    picks = route.reshape(rows_here)
    expert_ids = jnp.arange(experts, dtype=jnp.int32)
    member = (picks[:, None] == expert_ids[None, :]).astype(jnp.int32)
    earlier = jnp.cumsum(member, axis=0) - member
    slot_ids = jnp.sum(earlier * member, axis=1)
    target = picks * capacity + slot_ids
    slot_range = jnp.arange(experts * capacity, dtype=jnp.int32)
    placing = ((slot_range[:, None] == target[None, :]) & (slot_ids < capacity)[None, :]).astype(
        jnp.bfloat16
    )
    gate, gate_pull = jax.vjp(
        partial(route_gate, picked=member.astype(jnp.float32)),
        normed_two,
        route_weight,
        expert_embed,
    )
    sent = jnp.dot(
        placing, normed_two.astype(jnp.bfloat16), preferred_element_type=jnp.float32
    ).astype(jnp.bfloat16)
    received = lax.all_to_all(
        pair_copy(sent.reshape(experts, capacity, features)),
        "expert",
        split_axis=0,
        concat_axis=0,
        tiled=True,
    )
    recv_rows = received.shape[0] * capacity
    slot_block = received.reshape(recv_rows, features)
    up = jnp.dot(slot_block, up_weight[0], preferred_element_type=jnp.float32)
    active, act_pull = jax.vjp(gelu_exact, up)
    active_low = active.astype(jnp.bfloat16)
    returned = lax.dot_general(
        active_low, down_weight[0], contract_cols, preferred_element_type=jnp.float32
    )
    back = lax.all_to_all(
        returned.reshape(received.shape).astype(jnp.bfloat16),
        "expert",
        split_axis=0,
        concat_axis=0,
        tiled=True,
    ).astype(jnp.float32)
    back_low = pair_total(back).astype(jnp.bfloat16)
    mixture = lax.dot_general(
        placing,
        back_low.reshape(experts * capacity, features),
        contract_rows,
        preferred_element_type=jnp.float32,
    )
    result = hidden + gate[:, None] * mixture
    grad_out = out_grad.astype(jnp.float32).reshape(rows_here, features) * masked.reshape(
        rows_here, 1
    ).astype(jnp.float32)
    grad_gate = jnp.sum(grad_out * mixture, axis=1)
    grad_mixture = (gate[:, None] * grad_out).astype(jnp.bfloat16)
    grad_sent = jnp.dot(placing, grad_mixture, preferred_element_type=jnp.float32).astype(
        jnp.bfloat16
    )
    grad_received = lax.all_to_all(
        pair_copy(grad_sent.reshape(experts, capacity, features)),
        "expert",
        split_axis=0,
        concat_axis=0,
        tiled=True,
    )
    grad_rows_in = grad_received.reshape(recv_rows, features)
    grad_active = jnp.dot(grad_rows_in, down_weight[0], preferred_element_type=jnp.float32)
    grad_up = act_pull(grad_active)[0].astype(jnp.bfloat16)
    down_full = lax.dot_general(
        grad_rows_in, active_low, contract_rows, preferred_element_type=jnp.float32
    )
    up_full = lax.dot_general(
        slot_block, grad_up, contract_rows, preferred_element_type=jnp.float32
    )
    grad_slots = lax.dot_general(
        grad_up, up_weight[0], contract_cols, preferred_element_type=jnp.float32
    )
    up_weight_grad, down_weight_grad = (
        lax.psum_scatter(
            up_full.astype(jnp.bfloat16), "tensor", scatter_dimension=1, tiled=True
        ).astype(jnp.float32),
        lax.psum_scatter(
            down_full.astype(jnp.bfloat16), "tensor", scatter_dimension=1, tiled=True
        ).astype(jnp.float32),
    )
    grad_back = lax.all_to_all(
        grad_slots.reshape(received.shape).astype(jnp.bfloat16),
        "expert",
        split_axis=0,
        concat_axis=0,
        tiled=True,
    ).astype(jnp.float32)
    grad_back_low = pair_total(grad_back).astype(jnp.bfloat16)
    grad_normed = lax.dot_general(
        placing,
        grad_back_low.reshape(experts * capacity, features),
        contract_rows,
        preferred_element_type=jnp.float32,
    )
    grad_from_gate, route_weight_grad, embed_grad = gate_pull(grad_gate)
    grad_hidden_norm, norm2_grad = norm_two_pull(grad_normed + grad_from_gate)
    grad_hidden = grad_out + grad_hidden_norm
    grad_shard = grad_hidden.astype(jnp.bfloat16).reshape(seq_count, shard_len, features)
    gradient_complete = lax.all_gather(grad_shard, "tensor", axis=1, tiled=True)
    out_proj_local = jnp.einsum(
        "wif,wij->fj", mixed_everything, gradient_complete, preferred_element_type=jnp.float32
    )
    grad_mixed = jnp.einsum(
        "abc,qc->abq", gradient_complete, output_weight, preferred_element_type=jnp.float32
    ).astype(jnp.bfloat16)
    grad_mixed = grad_mixed.reshape(seq_count, seq_len, head_count, HEAD)
    grad_seqs = []
    for sequence in range(seq_count):
        key_all = heads_view[1, sequence]
        value_all = heads_view[2, sequence]
        grad_key = jnp.zeros((seq_len, head_count, HEAD), jnp.float32)
        grad_value = jnp.zeros((seq_len, head_count, HEAD), jnp.float32)
        query_grads = []
        for start_row in range(0, seq_len, block):
            query_part, key_part, value_part = attend_backward(
                heads_view[0, sequence, start_row : start_row + block],
                key_all,
                value_all,
                grad_mixed[sequence, start_row : start_row + block],
                total_rows[sequence][:, start_row : start_row + block],
                score_scale,
            )
            query_grads.append(query_part)
            grad_key = grad_key + key_part
            grad_value = grad_value + value_part
        grad_seqs.append(
            jnp.stack([jnp.concatenate(query_grads, axis=0), grad_key, grad_value], axis=0)
        )
    gradient_projected = (
        jnp.stack(grad_seqs, axis=1).astype(jnp.bfloat16).reshape(3, seq_count, seq_len, channels)
    )
    projection_local = jnp.einsum(
        "pwe,apwu->aeu", collected_rows, gradient_projected, preferred_element_type=jnp.float32
    )
    query_key_value_gradient, out_proj_grad = lax.psum((projection_local, out_proj_local), "expert")
    piece = gradient_projected
    grad_normed_one = lax.psum_scatter(
        jnp.einsum(
            "kslh,kdh->lsd", piece, query_key_value_weight, preferred_element_type=jnp.float32
        ).astype(jnp.bfloat16),
        "tensor",
        scatter_dimension=0,
        tiled=True,
    ).astype(jnp.float32)
    grad_inputs_norm, norm1_grad = norm_one_pull(
        grad_normed_one.transpose(1, 0, 2).reshape(rows_here, features)
    )
    input_grad = grad_hidden + grad_inputs_norm
    loads_local = jnp.sum(member, axis=0).astype(jnp.float32)
    norm1_grad, norm2_grad, route_weight_grad, embed_grad, loads = lax.psum(
        (norm1_grad, norm2_grad, route_weight_grad, embed_grad, loads_local), ("tensor", "expert")
    )
    return (
        result.reshape(seq_count, shard_len, features),
        input_grad.reshape(seq_count, shard_len, features),
        loads,
        norm1_grad,
        query_key_value_gradient,
        out_proj_grad,
        norm2_grad,
        route_weight_grad,
        embed_grad,
        up_weight_grad[None],
        down_weight_grad[None],
    )


def solution(mesh):
    return jax.shard_map(
        body,
        mesh=mesh,
        in_specs=(
            P("expert", "tensor", None),
            P("expert", "tensor", None),
            P("expert", "tensor"),
            P("expert", "tensor", None),
            P(),
            P(None, None, "tensor"),
            P("tensor", None),
            P(),
            P(),
            P(),
            P("expert", None, None),
            P("expert", None, None),
        ),
        out_specs=(
            P("expert", "tensor", None),
            P("expert", "tensor", None),
            P(),
            P(),
            P(None, None, "tensor"),
            P("tensor", None),
            P(),
            P(),
            P(),
            P("expert", None, "tensor"),
            P("expert", None, "tensor"),
        ),
        check_vma=False,
    )
```

profile of v0, /device:TPU:0, one launch (start us, length us, event | category | flops | bytes accessed | tf_op | source)
XLA Modules:
  0.0 632.9 jit_solution(8095519388316317315)
XLA Ops:
  12.0 2.3 fusion.75
  14.4 46.8 %all-gather.3.cloned.1.call-done = bf16[2,1024,768]{2,1,0:T(8,128)(2,1)} async-done(((bf16[2,256,768]{2,1,0:T(8,128)(2,1)}), bf16[2,1024,768]{2,1,0:T(8,128)(2,1)}) %all-gather.3.cloned.1.call-update) | async-done | bytes 3145744 | tf_op jit(solution)/shard_map/all_gather | solution.py:107
  61.2 3.9 fusion.49
  76.9 1.8 fusion.107
  82.7 3.7 convolution_bitcast_fusion
  89.4 67.4 %reduce-scatter.9.cloned.1.call-done = f32[256,2,768]{2,0,1:T(8,128)} async-done(((f32[1024,2,768]{2,0,1:T(8,128)}), f32[256,2,768]{2,0,1:T(8,128)}) %reduce-scatter.9.cloned.1.call-update) | async-done | bytes 1572880 | tf_op jit(solution)/shard_map/reduce_scatter | solution.py:134
  156.8 1.8 fusion.113
  161.4 42.2 %all_to_all.20 = bf16[8,128,768]{2,1,0:T(8,128)(2,1)S(1)} all-to-all(bf16[8,128,768]{2,1,0:T(8,128)(2,1)S(1)} %bitcast.361), channel_id=1, replica_groups=mesh['tensor'=4,'expert'=8] {'expert'}, dimensions={0} | all-to-all | bytes 3145728 | tf_op jit(solution)/shard_map/all_to_all | solution.py:161
  203.7 18.1 %multiply_convert_fusion.4 = (bf16[1024,1536]{1,0:T(8,128)(2,1)S(1)}, f32[1024,1536]{1,0:T(8,128)}, f32[1024,1536]{1,0:T(8,128)}) fusion(bf16[1024,768]{1,0:T(8,128)(2,1)S(1)} %bitcast.378, bf16[1,768,1536]{2,1,0:T(8,128)(2,1)S(1)} %copy-done), kind=kOutput, calls=%fused_computation.16 | convolution fusion | flops 2518155264 | bytes 19660800 | tf_op jit(solution)/shard_map/dot_general | solution.py:170
  221.8 1.7 copy-done.126
  223.5 3.7 fusion.52
  227.2 4.9 all-to-all-start.1
  232.8 3.1 multiply_reduce_fusion.12
  237.4 32.5 %all-to-all-done.1 = bf16[8,128,768]{2,1,0:T(8,128)(2,1)} async-done(((bf16[8,128,768]{2,1,0:T(8,128)(2,1)}), bf16[8,128,768]{2,1,0:T(8,128)(2,1)}, u32[]{:S(2)}, u32[]{:S(2)}) %all-to-all-start.1) | async-done | bytes 1572896 | tf_op jit(solution)/shard_map/all_to_all | solution.py:176
  269.9 1.6 bitcast_reduce_fusion.1
  271.6 2.4 fusion.66
  275.7 40.4 %all_to_all.21 = bf16[8,128,768]{2,1,0:T(8,128)(2,1)S(1)} all-to-all(bf16[8,128,768]{2,1,0:T(8,128)(2,1)S(1)} %bitcast.362), channel_id=1, replica_groups=mesh['tensor'=4,'expert'=8] {'expert'}, dimensions={0} | all-to-all | bytes 3145728 | tf_op jit(solution)/shard_map/all_to_all | solution.py:199
  316.1 7.5 %add_convert_fusion = bf16[1024,1536]{1,0:T(8,128)(2,1)S(1)} fusion(f32[1024,1536]{1,0:T(8,128)} %get-tuple-element.29, f32[1024,1536]{1,0:T(8,128)} %get-tuple-element.47, bf16[1024,768]{1,0:T(8,128)(2,1)S(1)} %bitcast.380, bf16[1,768,1536]{2,1,0:T(8,128)(2,1)S(1)} %copy-done.123), kind=kOutput, calls=%fused_computation.15 | convolution fusion | flops 2437939200 | bytes 19660800 | tf_op jit(solution)/shard_map/dot_general | solution.py:207
  323.6 1.7 copy-done.127
  325.3 3.7 fusion.55
  329.1 4.5 all-to-all-start.3
  334.6 36.7 %all-to-all-done.3 = bf16[8,128,768]{2,1,0:T(8,128)(2,1)} async-done(((bf16[8,128,768]{2,1,0:T(8,128)(2,1)}), bf16[8,128,768]{2,1,0:T(8,128)(2,1)}, u32[]{:S(2)}, u32[]{:S(2)}) %all-to-all-start.3) | async-done | bytes 1572896 | tf_op jit(solution)/shard_map/all_to_all | solution.py:226
  371.3 1.6 bitcast_reduce_fusion
  374.5 3.2 multiply_reduce_fusion.8
  377.7 1.8 fusion.200
  382.1 6.4 %convolution_convert_fusion = bf16[768,1536]{1,0:T(8,128)(2,1)} fusion(bf16[1024,768]{1,0:T(8,128)(2,1)} %bitcast.381, bf16[1024,1536]{1,0:T(8,128)(2,1)} %copy-done.126), kind=kOutput, calls=%fused_computation.50 | convolution fusion | flops 2417098752 | bytes 7077888 | tf_op jit(solution)/shard_map/dot_general | solution.py:209
  388.6 4.4 copy.71
  393.2 6.4 %convolution_convert_fusion.1 = bf16[768,1536]{1,0:T(8,128)(2,1)} fusion(bf16[1024,768]{1,0:T(8,128)(2,1)} %bitcast.379, bf16[1024,1536]{1,0:T(8,128)(2,1)} %copy-done.127), kind=kOutput, calls=%fused_computation.51 | convolution fusion | flops 2417098752 | bytes 7077888 | tf_op jit(solution)/shard_map/dot_general | solution.py:212
  399.6 4.3 copy.69
  404.0 19.9 %all-gather.5.cloned.1.call-done = bf16[2,1024,768]{2,1,0:T(8,128)(2,1)} async-done(((bf16[2,256,768]{2,1,0:T(8,128)(2,1)}), bf16[2,1024,768]{2,1,0:T(8,128)(2,1)}) %all-gather.5.cloned.1.call-update) | async-done | bytes 3145744 | tf_op jit(solution)/shard_map/all_gather | solution.py:244
  423.9 3.2 convolution_convert_fusion.2
  427.1 4.3 multiply_reduce_fusion
  431.4 4.2 multiply_convert_fusion
  436.7 2.1 multiply_reduce_fusion.1
  441.6 3.8 multiply_reduce_fusion.2
  445.4 3.9 multiply_convert_fusion.2
  450.3 3.8 multiply_reduce_fusion.3
  454.9 3.8 multiply_convert_fusion.3
  470.5 4.1 fusion.22
  476.9 1.8 fusion.121
  480.2 24.4 %reduce-scatter.13.cloned.1.call-done = bf16[384,768]{1,0:T(8,128)(2,1)} async-done(((bf16[1536,768]{1,0:T(8,128)(2,1)}), bf16[384,768]{1,0:T(8,128)(2,1)}) %reduce-scatter.13.cloned.1.call-update) | async-done | bytes 589840
  510.4 3.4 fusion.78
  513.9 37.5 %reduce-scatter.11.cloned.1.call-done = bf16[256,2,768]{2,0,1:T(8,128)(2,1)} async-done(((bf16[1024,2,768]{2,0,1:T(8,128)(2,1)}), bf16[256,2,768]{2,0,1:T(8,128)(2,1)}) %reduce-scatter.11.cloned.1.call-update) | async-done | bytes 786448 | tf_op jit(solution)/shard_map/reduce_scatter | solution.py:282
  553.0 2.1 fusion.70
  555.1 41.3 %all-reduce = (f32[4]{0:T(128)}, f32[768]{0:T(1024)}, f32[768]{0:T(1024)}, f32[768,16]{0,1:T(8,128)}, f32[4,16]{1,0:T(4,128)}) all-reduce(f32[4]{0:T(128)S(1)} %copy-done.113, f32[768]{0:T(1024)S(1)} %get-tuple-element.13, f32[768]{0:T(1024)S(1)} %copy-done.93, ...), channel_id=1, replica_groups=mesh['tensor'=4,'expert'=8] {'tensor','expert'}, use_global_device_ids=true, to_apply=%region_36.37 | all-reduce | flops 13892 | bytes 111136 | tf_op jit(solution)/shard_map/psum | solution.py:295
  596.4 3.3 fusion.59
  599.8 22.2 %all-reduce.4.cloned.1.call-done = (f32[3,768,192]{1,2,0:T(8,128)}, f32[192,768]{1,0:T(8,128)}) async-done(((f32[3,768,192]{1,2,0:T(8,128)}, f32[192,768]{1,0:T(8,128)}), (f32[3,768,192]{1,2,0:T(8,128)}, f32[192,768]{1,0:T(8,128)})) %all-reduce.4.cloned.1.call-update) | async-done | bytes 2359312 | tf_op jit(solution)/shard_map/psum | solution.py:280
  622.0 2.9 copy.92
  (378 shorter events, 64.2 us)
Async XLA Ops:
  7.2 196.5 %copy-start = (bf16[1,768,1536]{2,1,0:T(8,128)(2,1)S(1)}, bf16[1,768,1536]{2,1,0:T(8,128)(2,1)}, u32[]{:S(2)}) copy-start(bf16[1,768,1536]{2,1,0:T(8,128)(2,1)} %param.22) | copy-start | bytes 7077892
  7.2 54.0 %copy-start.124 = (bf16[3,768,192]{1,2,0:T(8,128)(2,1)S(1)}, bf16[3,768,192]{1,2,0:T(8,128)(2,1)}, u32[]{:S(2)}) copy-start(bf16[3,768,192]{1,2,0:T(8,128)(2,1)} %param.17) | copy-start | bytes 2654212
  7.2 54.0 %all-gather.3.cloned.1.call-start = ((), (), s32[]{:S(2)}) async-start(), calls=%async_computation.8 | async-start | bytes 3932160 | tf_op jit(solution)/shard_map/all_gather | solution.py:107
  14.4 142.4 %reduce-scatter.9.cloned.1.call-start = ((), (), s32[]{:S(2)}) async-start(), calls=%async_computation.9 | async-start | bytes 7864320 | tf_op jit(solution)/shard_map/reduce_scatter | solution.py:134
  65.1 14.9 %copy-start.10 = (bf16[2,1024,3,192]{1,3,2,0:T(8,128)(2,1)}, bf16[2,1024,3,192]{1,3,2,0:T(8,128)(2,1)S(1)}, u32[]{:S(2)}) copy-start(bf16[2,1024,3,192]{1,3,2,0:T(8,128)(2,1)S(1)} %fusion.49) | copy-start | bytes 7077892
  68.5 8.4 %copy-start.3 = (f32[3,512,1024]{2,1,0:T(8,128)}, f32[3,512,1024]{2,1,0:T(8,128)S(1)}, u32[]{:S(2)}) copy-start(f32[3,512,1024]{2,1,0:T(8,128)S(1)} %get-tuple-element.42) | copy-start | bytes 18874372
  68.5 8.4 %copy-start.46 = (f32[3,512]{1,0:T(4,128)}, f32[3,512]{1,0:T(4,128)S(1)}, u32[]{:S(2)}) copy-start(f32[3,512]{1,0:T(4,128)S(1)} %get-tuple-element.41) | copy-start | bytes 18436
  69.6 10.4 %copy-start.2 = (f32[3,512,1024]{2,1,0:T(8,128)}, f32[3,512,1024]{2,1,0:T(8,128)S(1)}, u32[]{:S(2)}) copy-start(f32[3,512,1024]{2,1,0:T(8,128)S(1)} %get-tuple-element.46) | copy-start | bytes 18874372
  69.6 10.4 %copy-start.48 = (f32[3,512]{1,0:T(4,128)}, f32[3,512]{1,0:T(4,128)S(1)}, u32[]{:S(2)}) copy-start(f32[3,512]{1,0:T(4,128)S(1)} %get-tuple-element.45) | copy-start | bytes 18436
  86.4 70.4 %copy-start.6 = (bf16[2,256,768]{2,1,0:T(8,128)(2,1)S(1)}, bf16[2,256,768]{2,1,0:T(8,128)(2,1)}, u32[]{:S(2)}) copy-start(bf16[2,256,768]{2,1,0:T(8,128)(2,1)} %param.12) | copy-start | bytes 2359300
  89.4 69.9 %copy-start.106 = (pred[512]{0:T(512)(128)(4,1)}, pred[512]{0:T(512)(128)(4,1)S(1)}, u32[]{:S(2)}) copy-start(pred[512]{0:T(512)(128)(4,1)S(1)} %broadcast_compare_fusion) | copy-start | bytes 1540
  89.4 182.1 %copy-start.105 = (s32[512]{0:T(512)}, s32[512]{0:T(512)S(1)}, u32[]{:S(2)}) copy-start(s32[512]{0:T(512)S(1)} %multiply_add_fusion.1) | copy-start | bytes 6148
  158.6 74.2 %copy-start.56 = (f32[1,2,2,128]{3,1,2,0:T(2,128)}, f32[1,2,2,128]{3,1,2,0:T(2,128)S(1)}, u32[]{:S(2)}) copy-start(f32[1,2,2,128]{3,1,2,0:T(2,128)S(1)} %copy.81) | copy-start | bytes 6148
  159.1 73.7 %copy-start.59 = (f32[512]{0:T(512)}, f32[512]{0:T(512)S(1)}, u32[]{:S(2)}) copy-start(f32[512]{0:T(512)S(1)} %rsqrt.45) | copy-start | bytes 6148
  203.7 18.1 %copy-start.21 = (bf16[8,128,768]{2,1,0:T(8,128)(2,1)}, bf16[8,128,768]{2,1,0:T(8,128)(2,1)S(1)}, u32[]{:S(2)}) copy-start(bf16[8,128,768]{2,1,0:T(8,128)(2,1)S(1)} %all_to_all.20) | copy-start | bytes 4718596
  203.7 19.8 %copy-start.122 = (bf16[1,768,1536]{2,1,0:T(8,128)(2,1)S(1)}, bf16[1,768,1536]{2,1,0:T(8,128)(2,1)}, u32[]{:S(2)}) copy-start(bf16[1,768,1536]{2,1,0:T(8,128)(2,1)} %param.23) | copy-start | bytes 7077892
  227.2 44.3 %copy-start.14 = (bf16[2,256,768]{2,1,0:T(8,128)(2,1)S(1)}, bf16[2,256,768]{2,1,0:T(8,128)(2,1)}, u32[]{:S(2)}) copy-start(bf16[2,256,768]{2,1,0:T(8,128)(2,1)} %param.13) | copy-start | bytes 2359300
  227.2 42.7 %all-to-all-start.1 = ((bf16[8,128,768]{2,1,0:T(8,128)(2,1)}), bf16[8,128,768]{2,1,0:T(8,128)(2,1)}, u32[]{:S(2)}, u32[]{:S(2)}) async-start(bf16[8,128,768]{2,1,0:T(8,128)(2,1)} %fusion.52), calls=%async_computation.2 | async-start | bytes 3145728 | tf_op jit(solution)/shard_map/all_to_all | solution.py:176
  232.1 41.9 %copy-start.80 = (f32[1,2,2,128]{3,1,2,0:T(2,128)}, f32[1,2,2,128]{3,1,2,0:T(2,128)S(1)}, u32[]{:S(2)}) copy-start(f32[1,2,2,128]{3,1,2,0:T(2,128)S(1)} %copy.84) | copy-start | bytes 6148
  235.9 138.6 %copy-start.35 = (f32[512,16]{0,1:T(8,128)}, f32[512,16]{0,1:T(8,128)S(1)}, u32[]{:S(2)}) copy-start(f32[512,16]{0,1:T(8,128)S(1)} %get-tuple-element.49) | copy-start | bytes 98308
  236.5 39.0 %copy-start.82 = (f32[512]{0:T(512)}, f32[512]{0:T(512)S(1)}, u32[]{:S(2)}) copy-start(f32[512]{0:T(512)S(1)} %add_rsqrt_fusion) | copy-start | bytes 6148
  236.7 38.8 %copy-start.73 = (f32[512,4]{0,1:T(4,128)}, f32[512,4]{0,1:T(4,128)S(1)}, u32[]{:S(2)}) copy-start(f32[512,4]{0,1:T(4,128)S(1)} %get-tuple-element.51) | copy-start | bytes 24580
  237.3 38.2 %copy-start.90 = (f32[512]{0:T(512)}, f32[512]{0:T(512)S(1)}, u32[]{:S(2)}) copy-start(f32[512]{0:T(512)S(1)} %fusion.197) | copy-start | bytes 6148
  275.6 40.5 %copy-start.123 = (bf16[1,768,1536]{2,1,0:T(8,128)(2,1)S(1)}, bf16[1,768,1536]{2,1,0:T(8,128)(2,1)}, u32[]{:S(2)}) copy-start(bf16[1,768,1536]{2,1,0:T(8,128)(2,1)} %param.23) | copy-start | bytes 7077892
  316.1 7.5 %copy-start.22 = (bf16[8,128,768]{2,1,0:T(8,128)(2,1)}, bf16[8,128,768]{2,1,0:T(8,128)(2,1)S(1)}, u32[]{:S(2)}) copy-start(bf16[8,128,768]{2,1,0:T(8,128)(2,1)S(1)} %all_to_all.21) | copy-start | bytes 4718596
  329.1 42.3 %all-to-all-start.3 = ((bf16[8,128,768]{2,1,0:T(8,128)(2,1)}), bf16[8,128,768]{2,1,0:T(8,128)(2,1)}, u32[]{:S(2)}, u32[]{:S(2)}) async-start(bf16[8,128,768]{2,1,0:T(8,128)(2,1)} %fusion.55), calls=%async_computation.4 | async-start | bytes 3145728 | tf_op jit(solution)/shard_map/all_to_all | solution.py:226
  333.5 41.0 %copy-start.9 = (f32[512,768]{1,0:T(8,128)S(1)}, f32[512,768]{1,0:T(8,128)}, u32[]{:S(2)}) copy-start(f32[512,768]{1,0:T(8,128)} %copy-done.8) | copy-start | bytes 4718596
  333.5 90.4 %all-gather.5.cloned.1.call-start = ((), (), s32[]{:S(2)}) async-start(), calls=%async_computation.10 | async-start | bytes 3932160 | tf_op jit(solution)/shard_map/all_gather | solution.py:244
  334.0 43.7 %copy-start.40 = (f32[512,16]{0,1:T(8,128)}, f32[512,16]{0,1:T(8,128)S(1)}, u32[]{:S(2)}) copy-start(f32[512,16]{0,1:T(8,128)S(1)} %get-tuple-element.55) | copy-start | bytes 98308
  381.9 96.8 %reduce-scatter.15.cloned.1.call-start = ((), (), s32[]{:S(2)}) async-start(), calls=%async_computation.13 | async-start | bytes 2949120
  393.0 111.5 %reduce-scatter.13.cloned.1.call-start = ((), (), s32[]{:S(2)}) async-start(), calls=%async_computation.12 | async-start | bytes 2949120
  404.0 147.4 %reduce-scatter.11.cloned.1.call-start = ((), (), s32[]{:S(2)}) async-start(), calls=%async_computation.11 | async-start | bytes 3932160 | tf_op jit(solution)/shard_map/reduce_scatter | solution.py:282
  427.1 23.2 %copy-start.15 = (bf16[2,1024,192]{1,2,0:T(8,128)(2,1)}, bf16[2,1024,192]{1,2,0:T(8,128)(2,1)S(1)}, u32[]{:S(2)}) copy-start(bf16[2,1024,192]{1,2,0:T(8,128)(2,1)S(1)} %convolution_convert_fusion.2) | copy-start | bytes 2359300
  427.1 9.6 %slice-start.2 = ((s8[6291456]{0:T(1024)(128)(4,1)}), s8[4194304]{0:T(1024)(128)(4,1)S(1)}, s32[]{:S(2)}) async-start(s8[6291456]{0:T(1024)(128)(4,1)} %bitcast.333), calls=%async_computation.17 | async-start | bytes 8388608
  441.6 8.7 %slice-start = ((s8[6291456]{0:T(1024)(128)(4,1)}), s8[4194304]{0:T(1024)(128)(4,1)S(1)}, s32[]{:S(2)}) async-start(s8[6291456]{0:T(1024)(128)(4,1)} %bitcast.331), calls=%async_computation.15 | async-start | bytes 8388608
  474.9 147.1 %all-reduce.4.cloned.1.call-start = ((), (), s32[]{:S(2)}) async-start(), calls=%async_computation.14 | async-start | bytes 4718592 | tf_op jit(solution)/shard_map/psum | solution.py:280
  478.7 29.4 %copy-start.18 = (bf16[1024,3,64]{0,2,1:T(8,128)(2,1)S(1)}, bf16[1024,3,64]{0,2,1:T(8,128)(2,1)}, u32[]{:S(2)}) copy-start(bf16[1024,3,64]{0,2,1:T(8,128)(2,1)} %copy-done.17) | copy-start | bytes 1179652
  478.7 29.4 %copy-start.20 = (bf16[1024,3,64]{0,2,1:T(8,128)(2,1)S(1)}, bf16[1024,3,64]{0,2,1:T(8,128)(2,1)}, u32[]{:S(2)}) copy-start(bf16[1024,3,64]{0,2,1:T(8,128)(2,1)} %copy-done.19) | copy-start | bytes 1179652
  510.4 41.0 %copy-start.7 = (bf16[2,256,768]{2,1,0:T(8,128)(2,1)S(1)}, bf16[2,256,768]{2,1,0:T(8,128)(2,1)}, u32[]{:S(2)}) copy-start(bf16[2,256,768]{2,1,0:T(8,128)(2,1)} %param.12) | copy-start | bytes 2359300
  510.4 41.0 %copy-start.53 = (f32[768]{0:T(1024)S(1)}, f32[768]{0:T(1024)}, u32[]{:S(2)}) copy-start(f32[768]{0:T(1024)} %param.16) | copy-start | bytes 9220
  510.4 41.0 %copy-start.55 = (f32[2,256]{1,0:T(2,128)S(1)}, f32[2,256]{1,0:T(2,128)}, u32[]{:S(2)}) copy-start(f32[2,256]{1,0:T(2,128)} %copy-done.54) | copy-start | bytes 6148
  513.8 39.2 %copy-start.87 = (f32[2,256]{1,0:T(2,128)S(1)}, f32[2,256]{1,0:T(2,128)}, u32[]{:S(2)}) copy-start(f32[2,256]{1,0:T(2,128)} %copy-done.86) | copy-start | bytes 6148
  513.8 39.2 %copy-start.79 = (f32[2,256]{1,0:T(2,128)S(1)}, f32[2,256]{1,0:T(2,128)}, u32[]{:S(2)}) copy-start(f32[2,256]{1,0:T(2,128)} %copy-done.78) | copy-start | bytes 6148
  513.8 41.3 %copy-start.39 = (f32[768,16]{0,1:T(8,128)S(1)}, f32[768,16]{0,1:T(8,128)}, u32[]{:S(2)}) copy-start(f32[768,16]{0,1:T(8,128)} %fusion.121) | copy-start | bytes 147460
  513.8 41.3 %copy-start.93 = (f32[768]{0:T(1024)S(1)}, f32[768]{0:T(1024)}, u32[]{:S(2)}) copy-start(f32[768]{0:T(1024)} %get-tuple-element.11) | copy-start | bytes 9220
  513.8 41.3 %copy-start.104 = (f32[4,16]{1,0:T(4,128)S(1)}, f32[4,16]{1,0:T(4,128)}, u32[]{:S(2)}) copy-start(f32[4,16]{1,0:T(4,128)} %add_add_fusion.6) | copy-start | bytes 772
  513.8 41.3 %copy-start.113 = (f32[4]{0:T(128)S(1)}, f32[4]{0:T(128)}, u32[]{:S(2)}) copy-start(f32[4]{0:T(128)} %convert_element_type.207) | copy-start | bytes 52
  596.4 29.2 %copy-start.1 = (bf16[1,768,1536]{2,1,0:T(8,128)(2,1)S(1)}, bf16[1,768,1536]{2,1,0:T(8,128)(2,1)}, u32[]{:S(2)}) copy-start(bf16[1,768,1536]{2,1,0:T(8,128)(2,1)} %param.22) | copy-start | bytes 7077892
  (97 other events, 284.2 us)
Sparse Core Ops, SparseCore 0:
  14.5 46.6 all-gather.2
  86.5 70.2 reduce-scatter.8
  382.0 41.8 all-gather.4
  426.8 37.3 reduce-scatter.14
  467.1 37.3 reduce-scatter.12
  507.4 43.9 reduce-scatter.10
  554.4 67.4 all-reduce.3
where the time goes:
time: 643 us; the launch traced here: 633 us
  waiting for transfers between devices  288 us (45%)
  blocking collectives  124 us (19%)
  matrix products  118 us (18%)
  other arithmetic  48.2 us (7%)
  local copies, waits for them, and re-layouts  29.3 us (5%)
  between operations  16.3 us (3%)
  starting transfers between devices  9.77 us (2%)
    reduce_scatter x1, waiting for transfers between devices, body(): lax.psum_scatter(jnp.einsum('slh,hd->lsd', piece, output_weight, preferre...  67.4 us
    all_gather x1, waiting for transfers between devices, body(): collected_rows = lax.all_gather(normed_low, 'tensor', axis=1, tiled=True)  46.8 us
    all_to_all x1, blocking collectives, body(): lax.all_to_all(pair_copy(sent.reshape(experts, capacity, features)), 'exp...  42.2 us
    psum x1, blocking collectives, body(): lax.psum((norm1_grad, norm2_grad, route_weight_grad, embed_grad, loads_lo...  41.3 us
    all_to_all x1, blocking collectives, body(): lax.all_to_all(pair_copy(grad_sent.reshape(experts, capacity, features)),...  40.4 us
    reduce_scatter x1, waiting for transfers between devices, body(): lax.psum_scatter(jnp.einsum('kslh,kdh->lsd', piece, query_key_value_weigh...  37.5 us
    all_to_all x1, waiting for transfers between devices, body(): lax.all_to_all(grad_slots.reshape(received.shape).astype(jnp.bfloat16), '...  36.7 us
    all_to_all x1, waiting for transfers between devices, body(): lax.all_to_all(returned.reshape(received.shape).astype(jnp.bfloat16), 'ex...  32.5 us
  transfers between devices with their start and end apart: 9, of which 8 were waited for; matrix products, arithmetic and copies ran while one was open for 15% of the time, Pallas kernels for 0%

commit v1 on v0

--- a/solution.py
+++ b/solution.py
@@ -293,7 +293,8 @@
     input_grad = grad_hidden + grad_inputs_norm
     loads_local = jnp.sum(member, axis=0).astype(jnp.float32)
     norm1_grad, norm2_grad, route_weight_grad, embed_grad, loads = lax.psum(
-        (norm1_grad, norm2_grad, route_weight_grad, embed_grad, loads_local), ("tensor", "expert")
+        lax.psum((norm1_grad, norm2_grad, route_weight_grad, embed_grad, loads_local), "expert"),
+        "tensor",
     )
     return (
         result.reshape(seq_count, shard_len, features),

time: 643 us -> 643 us (level)
    psum x0 -> x1, blocking collectives: none -> 16.8 us  [body(): lax.psum(lax.psum((norm1_grad, norm2_grad, route_weight_grad, embed_grad,...]
    psum x1, blocking collectives: 41.3 us -> 29.9 us  [body(): lax.psum((norm1_grad, norm2_grad, route_weight_grad, embed_grad, loads_lo...]
where the time goes in v1:
time: 643 us; the launch traced here: 633 us
  waiting for transfers between devices  282 us (44%)
  blocking collectives  129 us (20%)
  matrix products  118 us (18%)
  other arithmetic  48.2 us (7%)
  local copies, waits for them, and re-layouts  29.4 us (5%)
  between operations  16.3 us (3%)
  starting transfers between devices  9.76 us (2%)
    reduce_scatter x1, waiting for transfers between devices, body(): lax.psum_scatter(jnp.einsum('slh,hd->lsd', piece, output_weight, preferre...  67.4 us
    all_gather x1, waiting for transfers between devices, body(): collected_rows = lax.all_gather(normed_low, 'tensor', axis=1, tiled=True)  46.8 us
    all_to_all x1, blocking collectives, body(): lax.all_to_all(pair_copy(sent.reshape(experts, capacity, features)), 'exp...  42.2 us
    all_to_all x1, blocking collectives, body(): lax.all_to_all(pair_copy(grad_sent.reshape(experts, capacity, features)),...  40.4 us
    reduce_scatter x1, waiting for transfers between devices, body(): lax.psum_scatter(jnp.einsum('kslh,kdh->lsd', piece, query_key_value_weigh...  37.5 us
    all_to_all x1, waiting for transfers between devices, body(): lax.all_to_all(grad_slots.reshape(received.shape).astype(jnp.bfloat16), '...  36.8 us
    all_to_all x1, waiting for transfers between devices, body(): lax.all_to_all(returned.reshape(received.shape).astype(jnp.bfloat16), 'ex...  32.5 us
    psum x1, blocking collectives, body(): lax.psum((norm1_grad, norm2_grad, route_weight_grad, embed_grad, loads_lo...  29.9 us
  transfers between devices with their start and end apart: 9, of which 8 were waited for; matrix products, arithmetic and copies ran while one was open for 15% of the time, Pallas kernels for 0%

profile of v1, /device:TPU:0, one launch (start us, length us, event | category | flops | bytes accessed | tf_op | source)
XLA Modules:
  0.0 633.1 jit_solution(13159970204793569793)
XLA Ops:
  12.0 2.3 fusion.75
  14.4 46.8 %all-gather.3.cloned.1.call-done = bf16[2,1024,768]{2,1,0:T(8,128)(2,1)} async-done(((bf16[2,256,768]{2,1,0:T(8,128)(2,1)}), bf16[2,1024,768]{2,1,0:T(8,128)(2,1)}) %all-gather.3.cloned.1.call-update) | async-done | bytes 3145744 | tf_op jit(solution)/shard_map/all_gather | solution.py:107
  61.2 3.9 fusion.49
  76.9 1.8 fusion.107
  82.7 3.7 convolution_bitcast_fusion
  89.4 67.4 %reduce-scatter.9.cloned.1.call-done = f32[256,2,768]{2,0,1:T(8,128)} async-done(((f32[1024,2,768]{2,0,1:T(8,128)}), f32[256,2,768]{2,0,1:T(8,128)}) %reduce-scatter.9.cloned.1.call-update) | async-done | bytes 1572880 | tf_op jit(solution)/shard_map/reduce_scatter | solution.py:134
  156.8 1.8 fusion.113
  161.4 42.2 %all_to_all.20 = bf16[8,128,768]{2,1,0:T(8,128)(2,1)S(1)} all-to-all(bf16[8,128,768]{2,1,0:T(8,128)(2,1)S(1)} %bitcast.361), channel_id=1, replica_groups=mesh['tensor'=4,'expert'=8] {'expert'}, dimensions={0} | all-to-all | bytes 3145728 | tf_op jit(solution)/shard_map/all_to_all | solution.py:161
  203.7 18.1 %multiply_convert_fusion.4 = (bf16[1024,1536]{1,0:T(8,128)(2,1)S(1)}, f32[1024,1536]{1,0:T(8,128)}, f32[1024,1536]{1,0:T(8,128)}) fusion(bf16[1024,768]{1,0:T(8,128)(2,1)S(1)} %bitcast.378, bf16[1,768,1536]{2,1,0:T(8,128)(2,1)S(1)} %copy-done), kind=kOutput, calls=%fused_computation.16 | convolution fusion | flops 2518155264 | bytes 19660800 | tf_op jit(solution)/shard_map/dot_general | solution.py:170
  221.8 1.7 copy-done.126
  223.5 3.7 fusion.52
  227.2 4.9 all-to-all-start.1
  232.9 3.1 multiply_reduce_fusion.12
  237.4 32.5 %all-to-all-done.1 = bf16[8,128,768]{2,1,0:T(8,128)(2,1)} async-done(((bf16[8,128,768]{2,1,0:T(8,128)(2,1)}), bf16[8,128,768]{2,1,0:T(8,128)(2,1)}, u32[]{:S(2)}, u32[]{:S(2)}) %all-to-all-start.1) | async-done | bytes 1572896 | tf_op jit(solution)/shard_map/all_to_all | solution.py:176
  269.9 1.6 bitcast_reduce_fusion.1
  271.6 2.4 fusion.66
  275.7 40.4 %all_to_all.21 = bf16[8,128,768]{2,1,0:T(8,128)(2,1)S(1)} all-to-all(bf16[8,128,768]{2,1,0:T(8,128)(2,1)S(1)} %bitcast.362), channel_id=1, replica_groups=mesh['tensor'=4,'expert'=8] {'expert'}, dimensions={0} | all-to-all | bytes 3145728 | tf_op jit(solution)/shard_map/all_to_all | solution.py:199
  316.1 7.5 %add_convert_fusion = bf16[1024,1536]{1,0:T(8,128)(2,1)S(1)} fusion(f32[1024,1536]{1,0:T(8,128)} %get-tuple-element.34, f32[1024,1536]{1,0:T(8,128)} %get-tuple-element.52, bf16[1024,768]{1,0:T(8,128)(2,1)S(1)} %bitcast.380, bf16[1,768,1536]{2,1,0:T(8,128)(2,1)S(1)} %copy-done.123), kind=kOutput, calls=%fused_computation.15 | convolution fusion | flops 2437939200 | bytes 19660800 | tf_op jit(solution)/shard_map/dot_general | solution.py:207
  323.6 1.6 copy-done.127
  325.3 3.7 fusion.55
  329.1 4.4 all-to-all-start.3
  334.6 36.8 %all-to-all-done.3 = bf16[8,128,768]{2,1,0:T(8,128)(2,1)} async-done(((bf16[8,128,768]{2,1,0:T(8,128)(2,1)}), bf16[8,128,768]{2,1,0:T(8,128)(2,1)}, u32[]{:S(2)}, u32[]{:S(2)}) %all-to-all-start.3) | async-done | bytes 1572896 | tf_op jit(solution)/shard_map/all_to_all | solution.py:226
  374.5 3.1 multiply_reduce_fusion.8
  377.7 1.8 fusion.200
  382.1 6.4 %convolution_convert_fusion = bf16[768,1536]{1,0:T(8,128)(2,1)} fusion(bf16[1024,768]{1,0:T(8,128)(2,1)} %bitcast.381, bf16[1024,1536]{1,0:T(8,128)(2,1)} %copy-done.126), kind=kOutput, calls=%fused_computation.50 | convolution fusion | flops 2417098752 | bytes 7077888 | tf_op jit(solution)/shard_map/dot_general | solution.py:209
  388.6 4.5 copy.71
  393.2 6.4 %convolution_convert_fusion.1 = bf16[768,1536]{1,0:T(8,128)(2,1)} fusion(bf16[1024,768]{1,0:T(8,128)(2,1)} %bitcast.379, bf16[1024,1536]{1,0:T(8,128)(2,1)} %copy-done.127), kind=kOutput, calls=%fused_computation.51 | convolution fusion | flops 2417098752 | bytes 7077888 | tf_op jit(solution)/shard_map/dot_general | solution.py:212
  399.6 4.3 copy.69
  404.0 19.9 %all-gather.5.cloned.1.call-done = bf16[2,1024,768]{2,1,0:T(8,128)(2,1)} async-done(((bf16[2,256,768]{2,1,0:T(8,128)(2,1)}), bf16[2,1024,768]{2,1,0:T(8,128)(2,1)}) %all-gather.5.cloned.1.call-update) | async-done | bytes 3145744 | tf_op jit(solution)/shard_map/all_gather | solution.py:244
  423.9 3.2 convolution_convert_fusion.2
  427.2 4.3 multiply_reduce_fusion
  431.5 4.2 multiply_convert_fusion
  436.8 2.1 multiply_reduce_fusion.1
  441.6 3.8 multiply_reduce_fusion.2
  445.4 3.9 multiply_convert_fusion.2
  450.4 3.8 multiply_reduce_fusion.3
  454.9 3.8 multiply_convert_fusion.3
  470.5 4.1 fusion.22
  476.9 1.8 fusion.121
  480.2 24.4 %reduce-scatter.13.cloned.1.call-done = bf16[384,768]{1,0:T(8,128)(2,1)} async-done(((bf16[1536,768]{1,0:T(8,128)(2,1)}), bf16[384,768]{1,0:T(8,128)(2,1)}) %reduce-scatter.13.cloned.1.call-update) | async-done | bytes 589840
  510.4 3.4 fusion.78
  513.9 37.5 %reduce-scatter.11.cloned.1.call-done = bf16[256,2,768]{2,0,1:T(8,128)(2,1)} async-done(((bf16[1024,2,768]{2,0,1:T(8,128)(2,1)}), bf16[256,2,768]{2,0,1:T(8,128)(2,1)}) %reduce-scatter.11.cloned.1.call-update) | async-done | bytes 786448 | tf_op jit(solution)/shard_map/reduce_scatter | solution.py:282
  553.1 2.1 fusion.70
  555.2 29.9 %all-reduce = (f32[4]{0:T(128)S(1)}, f32[768]{0:T(1024)S(1)}, f32[768]{0:T(1024)S(1)}, f32[768,16]{0,1:T(8,128)S(1)}, f32[4,16]{1,0:T(4,128)S(1)}) all-reduce(f32[4]{0:T(128)S(1)} %copy-done.113, f32[768]{0:T(1024)S(1)} %get-tuple-element.13, f32[768]{0:T(1024)S(1)} %copy-done.93, ...), channel_id=1, replica_groups=mesh['tensor'=4,'expert'=8] {'expert'}, use_global_device_ids=true, to_apply=%region_36.37 | all-reduce | flops 13892 | bytes 111136 | tf_op jit(solution)/shard_map/psum | solution.py:296
  585.1 16.8 %all-reduce.2 = (f32[4]{0:T(128)}, f32[768]{0:T(1024)}, f32[768]{0:T(1024)}, f32[768,16]{0,1:T(8,128)}, f32[4,16]{1,0:T(4,128)}) all-reduce(f32[4]{0:T(128)S(1)} %get-tuple-element.19, f32[768]{0:T(1024)S(1)} %get-tuple-element.20, f32[768]{0:T(1024)S(1)} %get-tuple-element.21, ...), channel_id=1, replica_groups=mesh['tensor'=4,'expert'=8] {'tensor'}, use_global_device_ids=true, to_apply=%region_37.38 | all-reduce | flops 13892 | bytes 111136 | tf_op jit(solution)/shard_map/psum | solution.py:295
  601.9 3.4 fusion.59
  605.2 16.9 %all-reduce.5.cloned.1.call-done = (f32[3,768,192]{1,2,0:T(8,128)}, f32[192,768]{1,0:T(8,128)}) async-done(((f32[3,768,192]{1,2,0:T(8,128)}, f32[192,768]{1,0:T(8,128)}), (f32[3,768,192]{1,2,0:T(8,128)}, f32[192,768]{1,0:T(8,128)})) %all-reduce.5.cloned.1.call-update) | async-done | bytes 2359312 | tf_op jit(solution)/shard_map/psum | solution.py:280
  622.1 2.9 copy.92
  (379 shorter events, 65.8 us)
Async XLA Ops:
  7.2 196.5 %copy-start = (bf16[1,768,1536]{2,1,0:T(8,128)(2,1)S(1)}, bf16[1,768,1536]{2,1,0:T(8,128)(2,1)}, u32[]{:S(2)}) copy-start(bf16[1,768,1536]{2,1,0:T(8,128)(2,1)} %param.22) | copy-start | bytes 7077892
  7.2 54.0 %copy-start.124 = (bf16[3,768,192]{1,2,0:T(8,128)(2,1)S(1)}, bf16[3,768,192]{1,2,0:T(8,128)(2,1)}, u32[]{:S(2)}) copy-start(bf16[3,768,192]{1,2,0:T(8,128)(2,1)} %param.17) | copy-start | bytes 2654212
  7.2 54.0 %all-gather.3.cloned.1.call-start = ((), (), s32[]{:S(2)}) async-start(), calls=%async_computation.8 | async-start | bytes 3932160 | tf_op jit(solution)/shard_map/all_gather | solution.py:107
  14.4 142.4 %reduce-scatter.9.cloned.1.call-start = ((), (), s32[]{:S(2)}) async-start(), calls=%async_computation.9 | async-start | bytes 7864320 | tf_op jit(solution)/shard_map/reduce_scatter | solution.py:134
  65.1 14.9 %copy-start.10 = (bf16[2,1024,3,192]{1,3,2,0:T(8,128)(2,1)}, bf16[2,1024,3,192]{1,3,2,0:T(8,128)(2,1)S(1)}, u32[]{:S(2)}) copy-start(bf16[2,1024,3,192]{1,3,2,0:T(8,128)(2,1)S(1)} %fusion.49) | copy-start | bytes 7077892
  68.5 8.4 %copy-start.3 = (f32[3,512,1024]{2,1,0:T(8,128)}, f32[3,512,1024]{2,1,0:T(8,128)S(1)}, u32[]{:S(2)}) copy-start(f32[3,512,1024]{2,1,0:T(8,128)S(1)} %get-tuple-element.47) | copy-start | bytes 18874372
  68.5 8.4 %copy-start.46 = (f32[3,512]{1,0:T(4,128)}, f32[3,512]{1,0:T(4,128)S(1)}, u32[]{:S(2)}) copy-start(f32[3,512]{1,0:T(4,128)S(1)} %get-tuple-element.46) | copy-start | bytes 18436
  69.6 10.4 %copy-start.2 = (f32[3,512,1024]{2,1,0:T(8,128)}, f32[3,512,1024]{2,1,0:T(8,128)S(1)}, u32[]{:S(2)}) copy-start(f32[3,512,1024]{2,1,0:T(8,128)S(1)} %get-tuple-element.51) | copy-start | bytes 18874372
  69.6 10.4 %copy-start.48 = (f32[3,512]{1,0:T(4,128)}, f32[3,512]{1,0:T(4,128)S(1)}, u32[]{:S(2)}) copy-start(f32[3,512]{1,0:T(4,128)S(1)} %get-tuple-element.50) | copy-start | bytes 18436
  86.4 70.4 %copy-start.6 = (bf16[2,256,768]{2,1,0:T(8,128)(2,1)S(1)}, bf16[2,256,768]{2,1,0:T(8,128)(2,1)}, u32[]{:S(2)}) copy-start(bf16[2,256,768]{2,1,0:T(8,128)(2,1)} %param.12) | copy-start | bytes 2359300
  89.4 69.9 %copy-start.106 = (pred[512]{0:T(512)(128)(4,1)}, pred[512]{0:T(512)(128)(4,1)S(1)}, u32[]{:S(2)}) copy-start(pred[512]{0:T(512)(128)(4,1)S(1)} %broadcast_compare_fusion) | copy-start | bytes 1540
  89.4 182.1 %copy-start.105 = (s32[512]{0:T(512)}, s32[512]{0:T(512)S(1)}, u32[]{:S(2)}) copy-start(s32[512]{0:T(512)S(1)} %multiply_add_fusion.1) | copy-start | bytes 6148
  158.6 74.3 %copy-start.56 = (f32[1,2,2,128]{3,1,2,0:T(2,128)}, f32[1,2,2,128]{3,1,2,0:T(2,128)S(1)}, u32[]{:S(2)}) copy-start(f32[1,2,2,128]{3,1,2,0:T(2,128)S(1)} %copy.81) | copy-start | bytes 6148
  159.1 73.7 %copy-start.59 = (f32[512]{0:T(512)}, f32[512]{0:T(512)S(1)}, u32[]{:S(2)}) copy-start(f32[512]{0:T(512)S(1)} %rsqrt.45) | copy-start | bytes 6148
  203.7 18.1 %copy-start.21 = (bf16[8,128,768]{2,1,0:T(8,128)(2,1)}, bf16[8,128,768]{2,1,0:T(8,128)(2,1)S(1)}, u32[]{:S(2)}) copy-start(bf16[8,128,768]{2,1,0:T(8,128)(2,1)S(1)} %all_to_all.20) | copy-start | bytes 4718596
  203.7 19.8 %copy-start.122 = (bf16[1,768,1536]{2,1,0:T(8,128)(2,1)S(1)}, bf16[1,768,1536]{2,1,0:T(8,128)(2,1)}, u32[]{:S(2)}) copy-start(bf16[1,768,1536]{2,1,0:T(8,128)(2,1)} %param.23) | copy-start | bytes 7077892
  227.2 44.3 %copy-start.14 = (bf16[2,256,768]{2,1,0:T(8,128)(2,1)S(1)}, bf16[2,256,768]{2,1,0:T(8,128)(2,1)}, u32[]{:S(2)}) copy-start(bf16[2,256,768]{2,1,0:T(8,128)(2,1)} %param.13) | copy-start | bytes 2359300
  227.2 42.7 %all-to-all-start.1 = ((bf16[8,128,768]{2,1,0:T(8,128)(2,1)}), bf16[8,128,768]{2,1,0:T(8,128)(2,1)}, u32[]{:S(2)}, u32[]{:S(2)}) async-start(bf16[8,128,768]{2,1,0:T(8,128)(2,1)} %fusion.52), calls=%async_computation.2 | async-start | bytes 3145728 | tf_op jit(solution)/shard_map/all_to_all | solution.py:176
  232.1 41.9 %copy-start.80 = (f32[1,2,2,128]{3,1,2,0:T(2,128)}, f32[1,2,2,128]{3,1,2,0:T(2,128)S(1)}, u32[]{:S(2)}) copy-start(f32[1,2,2,128]{3,1,2,0:T(2,128)S(1)} %copy.84) | copy-start | bytes 6148
  236.0 138.5 %copy-start.35 = (f32[512,16]{0,1:T(8,128)}, f32[512,16]{0,1:T(8,128)S(1)}, u32[]{:S(2)}) copy-start(f32[512,16]{0,1:T(8,128)S(1)} %get-tuple-element.54) | copy-start | bytes 98308
  236.6 39.0 %copy-start.82 = (f32[512]{0:T(512)}, f32[512]{0:T(512)S(1)}, u32[]{:S(2)}) copy-start(f32[512]{0:T(512)S(1)} %add_rsqrt_fusion) | copy-start | bytes 6148
  236.8 38.7 %copy-start.73 = (f32[512,4]{0,1:T(4,128)}, f32[512,4]{0,1:T(4,128)S(1)}, u32[]{:S(2)}) copy-start(f32[512,4]{0,1:T(4,128)S(1)} %get-tuple-element.56) | copy-start | bytes 24580
  237.4 38.1 %copy-start.90 = (f32[512]{0:T(512)}, f32[512]{0:T(512)S(1)}, u32[]{:S(2)}) copy-start(f32[512]{0:T(512)S(1)} %fusion.197) | copy-start | bytes 6148
  275.6 40.5 %copy-start.123 = (bf16[1,768,1536]{2,1,0:T(8,128)(2,1)S(1)}, bf16[1,768,1536]{2,1,0:T(8,128)(2,1)}, u32[]{:S(2)}) copy-start(bf16[1,768,1536]{2,1,0:T(8,128)(2,1)} %param.23) | copy-start | bytes 7077892
  316.1 7.5 %copy-start.22 = (bf16[8,128,768]{2,1,0:T(8,128)(2,1)}, bf16[8,128,768]{2,1,0:T(8,128)(2,1)S(1)}, u32[]{:S(2)}) copy-start(bf16[8,128,768]{2,1,0:T(8,128)(2,1)S(1)} %all_to_all.21) | copy-start | bytes 4718596
  329.1 42.3 %all-to-all-start.3 = ((bf16[8,128,768]{2,1,0:T(8,128)(2,1)}), bf16[8,128,768]{2,1,0:T(8,128)(2,1)}, u32[]{:S(2)}, u32[]{:S(2)}) async-start(bf16[8,128,768]{2,1,0:T(8,128)(2,1)} %fusion.55), calls=%async_computation.4 | async-start | bytes 3145728 | tf_op jit(solution)/shard_map/all_to_all | solution.py:226
  333.5 41.0 %copy-start.9 = (f32[512,768]{1,0:T(8,128)S(1)}, f32[512,768]{1,0:T(8,128)}, u32[]{:S(2)}) copy-start(f32[512,768]{1,0:T(8,128)} %copy-done.8) | copy-start | bytes 4718596
  333.5 90.4 %all-gather.5.cloned.1.call-start = ((), (), s32[]{:S(2)}) async-start(), calls=%async_computation.10 | async-start | bytes 3932160 | tf_op jit(solution)/shard_map/all_gather | solution.py:244
  334.0 43.7 %copy-start.40 = (f32[512,16]{0,1:T(8,128)}, f32[512,16]{0,1:T(8,128)S(1)}, u32[]{:S(2)}) copy-start(f32[512,16]{0,1:T(8,128)S(1)} %get-tuple-element.60) | copy-start | bytes 98308
  381.9 96.9 %reduce-scatter.15.cloned.1.call-start = ((), (), s32[]{:S(2)}) async-start(), calls=%async_computation.13 | async-start | bytes 2949120
  393.0 111.6 %reduce-scatter.13.cloned.1.call-start = ((), (), s32[]{:S(2)}) async-start(), calls=%async_computation.12 | async-start | bytes 2949120
  404.0 147.4 %reduce-scatter.11.cloned.1.call-start = ((), (), s32[]{:S(2)}) async-start(), calls=%async_computation.11 | async-start | bytes 3932160 | tf_op jit(solution)/shard_map/reduce_scatter | solution.py:282
  427.1 23.2 %copy-start.15 = (bf16[2,1024,192]{1,2,0:T(8,128)(2,1)}, bf16[2,1024,192]{1,2,0:T(8,128)(2,1)S(1)}, u32[]{:S(2)}) copy-start(bf16[2,1024,192]{1,2,0:T(8,128)(2,1)S(1)} %convolution_convert_fusion.2) | copy-start | bytes 2359300
  427.2 9.6 %slice-start.2 = ((s8[6291456]{0:T(1024)(128)(4,1)}), s8[4194304]{0:T(1024)(128)(4,1)S(1)}, s32[]{:S(2)}) async-start(s8[6291456]{0:T(1024)(128)(4,1)} %bitcast.333), calls=%async_computation.17 | async-start | bytes 8388608
  441.6 8.7 %slice-start = ((s8[6291456]{0:T(1024)(128)(4,1)}), s8[4194304]{0:T(1024)(128)(4,1)S(1)}, s32[]{:S(2)}) async-start(s8[6291456]{0:T(1024)(128)(4,1)} %bitcast.331), calls=%async_computation.15 | async-start | bytes 8388608
  474.9 147.3 %all-reduce.5.cloned.1.call-start = ((), (), s32[]{:S(2)}) async-start(), calls=%async_computation.14 | async-start | bytes 4718592 | tf_op jit(solution)/shard_map/psum | solution.py:280
  478.7 29.5 %copy-start.18 = (bf16[1024,3,64]{0,2,1:T(8,128)(2,1)S(1)}, bf16[1024,3,64]{0,2,1:T(8,128)(2,1)}, u32[]{:S(2)}) copy-start(bf16[1024,3,64]{0,2,1:T(8,128)(2,1)} %copy-done.17) | copy-start | bytes 1179652
  478.7 29.5 %copy-start.20 = (bf16[1024,3,64]{0,2,1:T(8,128)(2,1)S(1)}, bf16[1024,3,64]{0,2,1:T(8,128)(2,1)}, u32[]{:S(2)}) copy-start(bf16[1024,3,64]{0,2,1:T(8,128)(2,1)} %copy-done.19) | copy-start | bytes 1179652
  510.4 41.0 %copy-start.7 = (bf16[2,256,768]{2,1,0:T(8,128)(2,1)S(1)}, bf16[2,256,768]{2,1,0:T(8,128)(2,1)}, u32[]{:S(2)}) copy-start(bf16[2,256,768]{2,1,0:T(8,128)(2,1)} %param.12) | copy-start | bytes 2359300
  510.4 41.0 %copy-start.53 = (f32[768]{0:T(1024)S(1)}, f32[768]{0:T(1024)}, u32[]{:S(2)}) copy-start(f32[768]{0:T(1024)} %param.16) | copy-start | bytes 9220
  510.4 41.0 %copy-start.55 = (f32[2,256]{1,0:T(2,128)S(1)}, f32[2,256]{1,0:T(2,128)}, u32[]{:S(2)}) copy-start(f32[2,256]{1,0:T(2,128)} %copy-done.54) | copy-start | bytes 6148
  513.8 39.2 %copy-start.87 = (f32[2,256]{1,0:T(2,128)S(1)}, f32[2,256]{1,0:T(2,128)}, u32[]{:S(2)}) copy-start(f32[2,256]{1,0:T(2,128)} %copy-done.86) | copy-start | bytes 6148
  513.8 39.2 %copy-start.79 = (f32[2,256]{1,0:T(2,128)S(1)}, f32[2,256]{1,0:T(2,128)}, u32[]{:S(2)}) copy-start(f32[2,256]{1,0:T(2,128)} %copy-done.78) | copy-start | bytes 6148
  513.8 41.3 %copy-start.39 = (f32[768,16]{0,1:T(8,128)S(1)}, f32[768,16]{0,1:T(8,128)}, u32[]{:S(2)}) copy-start(f32[768,16]{0,1:T(8,128)} %fusion.121) | copy-start | bytes 147460
  513.8 41.3 %copy-start.93 = (f32[768]{0:T(1024)S(1)}, f32[768]{0:T(1024)}, u32[]{:S(2)}) copy-start(f32[768]{0:T(1024)} %get-tuple-element.11) | copy-start | bytes 9220
  513.8 41.3 %copy-start.104 = (f32[4,16]{1,0:T(4,128)S(1)}, f32[4,16]{1,0:T(4,128)}, u32[]{:S(2)}) copy-start(f32[4,16]{1,0:T(4,128)} %add_add_fusion.6) | copy-start | bytes 772
  513.9 41.3 %copy-start.113 = (f32[4]{0:T(128)S(1)}, f32[4]{0:T(128)}, u32[]{:S(2)}) copy-start(f32[4]{0:T(128)} %convert_element_type.207) | copy-start | bytes 52
  601.9 23.9 %copy-start.1 = (bf16[1,768,1536]{2,1,0:T(8,128)(2,1)S(1)}, bf16[1,768,1536]{2,1,0:T(8,128)(2,1)}, u32[]{:S(2)}) copy-start(bf16[1,768,1536]{2,1,0:T(8,128)(2,1)} %param.22) | copy-start | bytes 7077892
  (97 other events, 284.2 us)
Sparse Core Ops, SparseCore 0:
  14.5 46.6 all-gather.2
  86.5 70.2 reduce-scatter.8
  382.0 41.8 all-gather.4
  426.8 37.3 reduce-scatter.14
  467.2 37.3 reduce-scatter.12
  507.4 43.9 reduce-scatter.10
  554.5 67.6 all-reduce.4
